TPU v7x, 256 devices: a whole 4x4x8 slice. The times are simulated.
256 devices in a mesh: ctx: 8 (over x, y_lo), mp: 32 (over z, y_hi, core).
Axes of the slice: x: 4, y: 4 (y_hi: 2, y_lo: 2; y = y_hi * 2 + y_lo), z: 8, core: 2. Of those that a mesh axis runs over, the one named last changes fastest.
Arguments:
- residual_in: bfloat16 [4096, 8192], P('ctx', 'mp'), may hold values from -4 to 4
- query_rows: bfloat16 [4096, 8192], P('ctx', 'mp'), may hold values from -5 to 5
- key_rows: bfloat16 [4096, 8192], P('ctx', 'mp'), may hold values from -5 to 5
- value_rows: bfloat16 [4096, 8192], P('ctx', 'mp'), may hold values from -5 to 5
- out_weight: bfloat16 [8192, 8192], P('mp'), may hold values from -1 to 1
- gate_in: bfloat16 [4096, 8192], P('ctx', 'mp'), may hold values from -5 to 5
- gate_out: bfloat16 [4096, 8192], P('ctx', 'mp'), may hold values from -5 to 5
- short_taps: float32 [3, 8192], P(None, 'mp'), may hold values from -3 to 3
- decay_rates: float32 [16, 8192], P(None, 'mp'), may hold values from 4.8828126e-05 to 0.03
- residues: float32 [16, 8192], P(None, 'mp'), may hold values from -0.15 to 0.15
- skip_gain: float32 [8192], P('mp'), may hold values from -4 to 4
Outputs:
- attended: bfloat16 [4096, 8192], P('ctx', 'mp')
- hyena_out: bfloat16 [4096, 8192], P('ctx', 'mp')
All inputs are finite; a program needn't handle non-finite values.
Results may differ from a plain program's by a relative error of at most 0.02.
Values may be sent and summed in bfloat16 or wider, within the bound.
No kernel may reach another device: no remote copies, remote signals or barrier semaphores. Data moves between devices by JAX's collectives and lax.ppermute only.
A program may use at most 128 MiB of HBM per device.

v0:
```python
import jax
import jax.numpy as jnp
from jax import lax
from jax.sharding import PartitionSpec as P

HD = 128
BLOCK = 64
masked_floor = -1e30


def from_behind(value, axis, steps):
    count = lax.axis_size(axis)
    leading, last = (max(0, -steps), min(count, count - steps))
    return lax.ppermute(value, axis, [(source, source + steps) for source in range(leading, last)])


def modal_tables(decay_rates, residues, block):
    width = decay_rates.shape[1]
    lags = jnp.arange(block).astype(jnp.float32)
    lag_diff = lags[:, None] - lags[None, :]
    causal = lag_diff >= 0
    safe_diff = jnp.maximum(lag_diff, 0.0)

    def add_pole(total, pole):
        rate, residue = pole
        return (
            total + residue[None, None, :] * jnp.exp(-rate[None, None, :] * safe_diff[:, :, None]),
            None,
        )

    toeplitz, _ = lax.scan(
        add_pole, jnp.zeros((block, block, width), jnp.float32), (decay_rates, residues)
    )
    toeplitz = jnp.where(causal[:, :, None], toeplitz, 0.0)
    powers = jnp.exp(-decay_rates[None] * lags[:, None, None])
    inward = jnp.exp(-decay_rates[None] * (block - lags)[:, None, None])
    return (toeplitz, powers, inward)


def modal_conv(signal, decay_rates, residues, block):
    length, width = signal.shape
    toeplitz, powers, inward = modal_tables(decay_rates, residues, block)
    highest = lax.Precision.HIGHEST
    span = jnp.exp(-decay_rates * block)

    def modal_step(state, piece):
        local = jnp.einsum("ijc,jc->ic", toeplitz, piece, precision=highest)
        carried = jnp.einsum("inc,nc->ic", powers, residues * state, precision=highest)
        state = span * state + jnp.einsum("jnc,jc->nc", inward, piece, precision=highest)
        return (state, local + carried)

    start_state = jnp.zeros((decay_rates.shape[0], width), jnp.float32)
    state, result = lax.scan(modal_step, start_state, signal.reshape(length // block, block, width))
    return (result.reshape(length, width), state)


def attend(groups, key_rows, value_rows):
    width = key_rows.shape[1]
    heads = width // HD
    scale = HD ** (-0.5)
    query_sets = [(rows_q.reshape(rows_q.shape[0], heads, HD), pos_q) for rows_q, pos_q in groups]

    def update(state, queries, query_pos, keys_here, values_here, key_pos):
        running_top, running_total, running_sum = state
        scores = (
            jnp.einsum("qhd,khd->hqk", queries, keys_here, preferred_element_type=jnp.float32)
            * scale
        )
        allowed = (key_pos[None, :] <= query_pos[:, None])[None]
        masked = jnp.where(allowed, scores, masked_floor)
        new_top = jnp.maximum(running_top, jnp.max(masked, axis=-1))
        weights = jnp.where(allowed, jnp.exp(masked - new_top[..., None]), 0.0)
        rescale = jnp.exp(running_top - new_top)
        new_total = running_total * rescale + jnp.sum(weights, axis=-1)
        new_sum = running_sum * rescale[..., None] + jnp.einsum(
            "hqk,khd->hqd",
            weights.astype(jnp.bfloat16),
            values_here,
            preferred_element_type=jnp.float32,
        )
        return (new_top, new_total, new_sum)

    initial = tuple(
        (
            (
                jnp.full((heads, pos_q.shape[0]), masked_floor, jnp.float32),
                jnp.zeros((heads, pos_q.shape[0]), jnp.float32),
                jnp.zeros((heads, pos_q.shape[0], HD), jnp.float32),
            )
            for rows_q, pos_q in groups
        )
    )
    pieces = (
        lax.all_gather(key_rows, "ctx", axis=0, tiled=True),
        lax.all_gather(value_rows, "ctx", axis=0, tiled=True),
    )
    count = pieces[0].shape[0]
    blocks = count // count
    keys_all = pieces[0].reshape(blocks, count, heads, HD)
    values_all = pieces[1].reshape(blocks, count, heads, HD)
    index_rows = jnp.arange(count)
    pos_all = index_rows.reshape(blocks, count)

    def fold_step(states, block):
        keys_here, values_here, key_pos = block
        return (
            tuple(
                (
                    update(
                        states[g],
                        query_sets[g][0],
                        query_sets[g][1],
                        keys_here,
                        values_here,
                        key_pos,
                    )
                    for g in range(len(query_sets))
                )
            ),
            None,
        )

    result, _ = lax.scan(fold_step, initial, (keys_all, values_all, pos_all))
    return [(final[2] / final[1][..., None]).astype(jnp.bfloat16) for final in result]


def per_device(
    residual_in,
    query_rows,
    key_rows,
    value_rows,
    out_weight,
    gate_in,
    gate_out,
    short_taps,
    decay_rates,
    residues,
    skip_gain,
):
    rows = residual_in.shape[0]
    width = residual_in.shape[1]
    segment = lax.axis_index("ctx")
    query_pos = segment * rows + jnp.arange(rows)
    heads_out = attend([(query_rows, query_pos)], key_rows, value_rows)[0]
    heads = heads_out.shape[0]
    columns = out_weight.reshape(heads, HD, width * lax.axis_size("mp"))
    projected = lax.psum_scatter(
        jnp.einsum("hqd,hdc->cq", heads_out, columns, preferred_element_type=jnp.float32).astype(
            jnp.bfloat16
        ),
        "mp",
        scatter_dimension=0,
        tiled=True,
    ).astype(jnp.float32)
    attended = (residual_in.astype(jnp.float32) + projected.T).astype(jnp.bfloat16)
    taps = short_taps.shape[0]
    rim = from_behind(attended[rows - (taps - 1) :], "ctx", 1)
    extended = jnp.concatenate([rim, attended], axis=0).astype(jnp.float32)
    shortconv = jnp.zeros((rows, width), jnp.float32)
    for tap in range(taps):
        shortconv = (
            shortconv + short_taps[tap][None, :] * extended[taps - 1 - tap : taps - 1 - tap + rows]
        )
    signal = gate_in.astype(jnp.float32) * shortconv
    local, final_state = modal_conv(signal, decay_rates, residues, BLOCK)
    highest = lax.Precision.HIGHEST
    lag_rows = jnp.arange(rows).astype(jnp.float32)
    long_powers = residues[None] * jnp.exp(-decay_rates[None] * lag_rows[:, None, None])
    later_count = rows * lax.axis_size("ctx") // rows
    later_index = jnp.arange(later_count)
    gap = jnp.maximum((later_index - segment - 1) * rows, 0).astype(jnp.float32)
    factor = jnp.exp(-decay_rates[None] * gap[:, None, None])
    states = jnp.where((later_index > segment)[:, None, None], factor * final_state[None], 0.0)
    carried = lax.psum_scatter(
        jnp.einsum("inc,jnc->jic", long_powers, states, precision=highest)
        .reshape(rows * lax.axis_size("ctx"), width)
        .astype(jnp.bfloat16),
        "ctx",
        scatter_dimension=0,
        tiled=True,
    ).astype(jnp.float32)
    hyena_out = (
        gate_out.astype(jnp.float32) * (local + carried + skip_gain[None, :] * signal)
    ).astype(jnp.bfloat16)
    return (attended, hyena_out)


def solution(mesh):
    in_specs = (
        P("ctx", "mp"),
        P("ctx", "mp"),
        P("ctx", "mp"),
        P("ctx", "mp"),
        P("mp", None),
        P("ctx", "mp"),
        P("ctx", "mp"),
        P(None, "mp"),
        P(None, "mp"),
        P(None, "mp"),
        P("mp"),
    )
    out_specs = (P("ctx", "mp"), P("ctx", "mp"))
    return jax.shard_map(
        per_device, mesh=mesh, in_specs=in_specs, out_specs=out_specs, check_vma=False
    )
```

profile of v0, /device:TPU:26, one launch (start us, length us, event | category | flops | bytes accessed | tf_op | source)
XLA Modules:
  0.0 405.1 jit_solution(8935362246046610650)
XLA Ops:
  7.2 1.8 copy.19
  9.9 0.8 fusion.64
  10.8 0.7 fusion.63
  11.6 1.7 iota_compare_fusion
  13.2 54.2 %all-gather.3.cloned.1.call-done = bf16[4096,256]{0,1:T(8,128)(2,1)} async-done(((bf16[512,256]{0,1:T(8,128)(2,1)}), bf16[4096,256]{0,1:T(8,128)(2,1)}) %all-gather.3.cloned.1.call-update) | async-done | bytes 2097168 | tf_op jit(solution)/shard_map/all_gather | solution.py:94
  67.4 5.4 %fusion.6 = (f32[2,512]{1,0:T(2,128)S(1)}, f32[2,512,4096]{2,1,0:T(8,128)S(1)}) fusion(pred[512,4096]{1,0:T(8,128)(4,1)S(1)} %iota_compare_fusion, bf16[4096,2,128]{0,2,1:T(8,128)(2,1)} %bitcast.107, bf16[512,256]{1,0:T(8,128)(2,1)S(1)} %copy-done), kind=kOutput, calls=%fused_computation.17 | convolution fusion | flops 1086323712 | bytes 21237760 | tf_op jit(solution)/shard_map/while/body/eval_jaxpr/qhd,khd->hqk/dot_general | solution.py:66
  72.9 5.3 %fusion.7 = f32[2,512]{1,0:T(2,128)S(1)} fusion(f32[2,512,4096]{2,1,0:T(8,128)S(1)} %get-tuple-element.265, f32[2,512]{1,0:T(2,128)S(1)} %broadcast_maximum_fusion, pred[512,4096]{1,0:T(8,128)(4,1)S(1)} %iota_compare_fusion), kind=kLoop, calls=%fused_computation.18 | loop fusion | flops 20970496 | bytes 18882560 | tf_op jit(solution)/shard_map/while/body/eval_jaxpr/reduce_sum | solution.py:74
  78.6 44.5 %all-gather.5.cloned.1.call-done = bf16[4096,256]{1,0:T(8,128)(2,1)} async-done(((bf16[512,256]{1,0:T(8,128)(2,1)}), bf16[4096,256]{1,0:T(8,128)(2,1)}) %all-gather.5.cloned.1.call-update) | async-done | bytes 2097168 | tf_op jit(solution)/shard_map/all_gather | solution.py:95
  123.1 15.0 %fusion.9 = bf16[8192,512]{0,1:T(8,128)(2,1)} fusion(bf16[2,128,8192]{2,1,0:T(8,128)(2,1)} %bitcast.106, f32[2,512,4096]{2,1,0:T(8,128)} %copy-done.1, f32[2,512]{1,0:T(2,128)S(1)} %broadcast_maximum_fusion, pred[512,4096]{1,0:T(8,128)(4,1)S(1)} %iota_compare_fusion, f32[2,512]{1,0:T(2,128)S(1)} %get-tuple-element.263, ...), kind=kOutput, calls=%fused_computation.20 | convolution fusion | flops 3246784512 | bytes 33566720 | tf_op jit(solution)/shard_map/hqd,hdc->cq/dot_general | solution.py:148
  138.8 77.4 %while.32 = (s32[]{:T(128)}, f32[64,64,256]{2,1,0:T(8,128)}, f32[16,256]{1,0:T(8,128)S(1)}, f32[16,256]{1,0:T(8,128)}, f32[64]{0:T(128)S(1)}, /*index=5*/s32[]{:T(128)}, s32[]{:T(128)}) while((s32[]{:T(128)}, f32[64,64,256]{2,1,0:T(8,128)}, f32[16,256]{1,0:T(8,128)S(1)}, f32[16,256]{1,0:T(8,128)}, f32[64]{0:T(128)S(1)}, ...), condition=%wide.region_4.5_spmd.clone, body=%wide.region_3.4_spmd.clone.sunk | while | flops 4202755 | bytes 8427867 | solution.py:31
  139.6 2.5 select_add_fusion.2
  142.9 4.1 %select_add_fusion.2 = f32[64,64,256]{2,1,0:T(8,128)} fusion(f32[64,64,256]{2,1,0:T(8,128)} %get-tuple-element.374, f32[64,64]{1,0:T(8,128)S(1)} %subtract_maximum_fusion.2, f32[256]{0:T(256)S(1)} %bitcast.101, f32[256]{0:T(256)S(1)} %bitcast.102, pred[]{:T(512)S(6)} %compare.8), kind=kLoop, calls=%fused_computation.3.clone.1 | loop fusion | flops 4194304 | bytes 8407041 | tf_op jit(solution)/shard_map/while/body/eval_jaxpr/add | solution.py:27
  147.7 4.1 %select_add_fusion.2 = f32[64,64,256]{2,1,0:T(8,128)} fusion(f32[64,64,256]{2,1,0:T(8,128)} %get-tuple-element.374, f32[64,64]{1,0:T(8,128)S(1)} %subtract_maximum_fusion.2, f32[256]{0:T(256)S(1)} %bitcast.101, f32[256]{0:T(256)S(1)} %bitcast.102, pred[]{:T(512)S(6)} %compare.8), kind=kLoop, calls=%fused_computation.3.clone.1 | loop fusion | flops 4194304 | bytes 8407041 | tf_op jit(solution)/shard_map/while/body/eval_jaxpr/add | solution.py:27
  151.8 0.7 dynamic-slice_negate_fusion.2
  152.6 4.3 %select_add_fusion.2 = f32[64,64,256]{2,1,0:T(8,128)} fusion(f32[64,64,256]{2,1,0:T(8,128)} %get-tuple-element.374, f32[64,64]{1,0:T(8,128)S(1)} %subtract_maximum_fusion.2, f32[256]{0:T(256)S(1)} %bitcast.101, f32[256]{0:T(256)S(1)} %bitcast.102, pred[]{:T(512)S(6)} %compare.8), kind=kLoop, calls=%fused_computation.3.clone.1 | loop fusion | flops 4194304 | bytes 8407041 | tf_op jit(solution)/shard_map/while/body/eval_jaxpr/add | solution.py:27
  156.9 0.7 dynamic-slice_negate_fusion.2
  157.7 4.3 %select_add_fusion.2 = f32[64,64,256]{2,1,0:T(8,128)} fusion(f32[64,64,256]{2,1,0:T(8,128)} %get-tuple-element.374, f32[64,64]{1,0:T(8,128)S(1)} %subtract_maximum_fusion.2, f32[256]{0:T(256)S(1)} %bitcast.101, f32[256]{0:T(256)S(1)} %bitcast.102, pred[]{:T(512)S(6)} %compare.8), kind=kLoop, calls=%fused_computation.3.clone.1 | loop fusion | flops 4194304 | bytes 8407041 | tf_op jit(solution)/shard_map/while/body/eval_jaxpr/add | solution.py:27
  161.9 0.7 dynamic-slice_negate_fusion.2
  162.7 4.3 %select_add_fusion.2 = f32[64,64,256]{2,1,0:T(8,128)} fusion(f32[64,64,256]{2,1,0:T(8,128)} %get-tuple-element.374, f32[64,64]{1,0:T(8,128)S(1)} %subtract_maximum_fusion.2, f32[256]{0:T(256)S(1)} %bitcast.101, f32[256]{0:T(256)S(1)} %bitcast.102, pred[]{:T(512)S(6)} %compare.8), kind=kLoop, calls=%fused_computation.3.clone.1 | loop fusion | flops 4194304 | bytes 8407041 | tf_op jit(solution)/shard_map/while/body/eval_jaxpr/add | solution.py:27
  167.8 4.3 %select_add_fusion.2 = f32[64,64,256]{2,1,0:T(8,128)} fusion(f32[64,64,256]{2,1,0:T(8,128)} %get-tuple-element.374, f32[64,64]{1,0:T(8,128)S(1)} %subtract_maximum_fusion.2, f32[256]{0:T(256)S(1)} %bitcast.101, f32[256]{0:T(256)S(1)} %bitcast.102, pred[]{:T(512)S(6)} %compare.8), kind=kLoop, calls=%fused_computation.3.clone.1 | loop fusion | flops 4194304 | bytes 8407041 | tf_op jit(solution)/shard_map/while/body/eval_jaxpr/add | solution.py:27
  172.8 4.3 %select_add_fusion.2 = f32[64,64,256]{2,1,0:T(8,128)} fusion(f32[64,64,256]{2,1,0:T(8,128)} %get-tuple-element.374, f32[64,64]{1,0:T(8,128)S(1)} %subtract_maximum_fusion.2, f32[256]{0:T(256)S(1)} %bitcast.101, f32[256]{0:T(256)S(1)} %bitcast.102, pred[]{:T(512)S(6)} %compare.8), kind=kLoop, calls=%fused_computation.3.clone.1 | loop fusion | flops 4194304 | bytes 8407041 | tf_op jit(solution)/shard_map/while/body/eval_jaxpr/add | solution.py:27
  177.9 4.3 %select_add_fusion.2 = f32[64,64,256]{2,1,0:T(8,128)} fusion(f32[64,64,256]{2,1,0:T(8,128)} %get-tuple-element.374, f32[64,64]{1,0:T(8,128)S(1)} %subtract_maximum_fusion.2, f32[256]{0:T(256)S(1)} %bitcast.101, f32[256]{0:T(256)S(1)} %bitcast.102, pred[]{:T(512)S(6)} %compare.8), kind=kLoop, calls=%fused_computation.3.clone.1 | loop fusion | flops 4194304 | bytes 8407041 | tf_op jit(solution)/shard_map/while/body/eval_jaxpr/add | solution.py:27
  182.9 4.1 %select_add_fusion.2 = f32[64,64,256]{2,1,0:T(8,128)} fusion(f32[64,64,256]{2,1,0:T(8,128)} %get-tuple-element.374, f32[64,64]{1,0:T(8,128)S(1)} %subtract_maximum_fusion.2, f32[256]{0:T(256)S(1)} %bitcast.101, f32[256]{0:T(256)S(1)} %bitcast.102, pred[]{:T(512)S(6)} %compare.8), kind=kLoop, calls=%fused_computation.3.clone.1 | loop fusion | flops 4194304 | bytes 8407041 | tf_op jit(solution)/shard_map/while/body/eval_jaxpr/add | solution.py:27
  187.7 4.1 %select_add_fusion.2 = f32[64,64,256]{2,1,0:T(8,128)} fusion(f32[64,64,256]{2,1,0:T(8,128)} %get-tuple-element.374, f32[64,64]{1,0:T(8,128)S(1)} %subtract_maximum_fusion.2, f32[256]{0:T(256)S(1)} %bitcast.101, f32[256]{0:T(256)S(1)} %bitcast.102, pred[]{:T(512)S(6)} %compare.8), kind=kLoop, calls=%fused_computation.3.clone.1 | loop fusion | flops 4194304 | bytes 8407041 | tf_op jit(solution)/shard_map/while/body/eval_jaxpr/add | solution.py:27
  192.6 4.2 %select_add_fusion.2 = f32[64,64,256]{2,1,0:T(8,128)} fusion(f32[64,64,256]{2,1,0:T(8,128)} %get-tuple-element.374, f32[64,64]{1,0:T(8,128)S(1)} %subtract_maximum_fusion.2, f32[256]{0:T(256)S(1)} %bitcast.101, f32[256]{0:T(256)S(1)} %bitcast.102, pred[]{:T(512)S(6)} %compare.8), kind=kLoop, calls=%fused_computation.3.clone.1 | loop fusion | flops 4194304 | bytes 8407041 | tf_op jit(solution)/shard_map/while/body/eval_jaxpr/add | solution.py:27
  197.6 4.1 %select_add_fusion.2 = f32[64,64,256]{2,1,0:T(8,128)} fusion(f32[64,64,256]{2,1,0:T(8,128)} %get-tuple-element.374, f32[64,64]{1,0:T(8,128)S(1)} %subtract_maximum_fusion.2, f32[256]{0:T(256)S(1)} %bitcast.101, f32[256]{0:T(256)S(1)} %bitcast.102, pred[]{:T(512)S(6)} %compare.8), kind=kLoop, calls=%fused_computation.3.clone.1 | loop fusion | flops 4194304 | bytes 8407041 | tf_op jit(solution)/shard_map/while/body/eval_jaxpr/add | solution.py:27
  202.4 4.1 %select_add_fusion.2 = f32[64,64,256]{2,1,0:T(8,128)} fusion(f32[64,64,256]{2,1,0:T(8,128)} %get-tuple-element.374, f32[64,64]{1,0:T(8,128)S(1)} %subtract_maximum_fusion.2, f32[256]{0:T(256)S(1)} %bitcast.101, f32[256]{0:T(256)S(1)} %bitcast.102, pred[]{:T(512)S(6)} %compare.8), kind=kLoop, calls=%fused_computation.3.clone.1 | loop fusion | flops 4194304 | bytes 8407041 | tf_op jit(solution)/shard_map/while/body/eval_jaxpr/add | solution.py:27
  207.3 4.1 %select_add_fusion.2 = f32[64,64,256]{2,1,0:T(8,128)} fusion(f32[64,64,256]{2,1,0:T(8,128)} %get-tuple-element.374, f32[64,64]{1,0:T(8,128)S(1)} %subtract_maximum_fusion.2, f32[256]{0:T(256)S(1)} %bitcast.101, f32[256]{0:T(256)S(1)} %bitcast.102, pred[]{:T(512)S(6)} %compare.8), kind=kLoop, calls=%fused_computation.3.clone.1 | loop fusion | flops 4194304 | bytes 8407041 | tf_op jit(solution)/shard_map/while/body/eval_jaxpr/add | solution.py:27
  212.1 4.1 %select_add_fusion.2 = f32[64,64,256]{2,1,0:T(8,128)} fusion(f32[64,64,256]{2,1,0:T(8,128)} %get-tuple-element.374, f32[64,64]{1,0:T(8,128)S(1)} %subtract_maximum_fusion.2, f32[256]{0:T(256)S(1)} %bitcast.101, f32[256]{0:T(256)S(1)} %bitcast.102, pred[]{:T(512)S(6)} %compare.8), kind=kLoop, calls=%fused_computation.3.clone.1 | loop fusion | flops 4194304 | bytes 8407041 | tf_op jit(solution)/shard_map/while/body/eval_jaxpr/add | solution.py:27
  216.2 4.0 broadcast_select_fusion
  220.2 72.1 %reduce-scatter.3.cloned.1.call-done = bf16[256,512]{0,1:T(8,128)(2,1)} async-done(((bf16[8192,512]{0,1:T(8,128)(2,1)}), bf16[256,512]{0,1:T(8,128)(2,1)}) %reduce-scatter.3.cloned.1.call-update) | async-done | bytes 262160 | tf_op jit(solution)/shard_map/reduce_scatter | solution.py:147
  292.3 1.0 fusion.49
  293.4 3.5 collective-permute-start
  296.9 0.8 copy.24
  297.7 0.8 copy.22
  299.1 32.8 %while.33 = (s32[]{:T(128)}, f32[16,256]{1,0:T(8,128)S(1)}, f32[8,64,256]{2,1,0:T(8,128)}, f32[16,256]{1,0:T(8,128)S(1)}, f32[8,64,256]{2,1,0:T(8,128)S(1)}, /*i...) while((s32[]{:T(128)}, f32[16,256]{1,0:T(8,128)S(1)}, ...), condition=%wide.region_6.7_spmd.clone.clone.clone, body=%wide.region_5.6_spmd.clone.clone.clone.sunk | while | flops 3665923 | bytes 4949123 | solution.py:53
  299.8 2.8 multiply_reduce_fusion.7
  303.9 2.8 multiply_reduce_fusion.7
  308.0 2.8 multiply_reduce_fusion.7
  312.1 2.8 multiply_reduce_fusion.7
  316.2 2.8 multiply_reduce_fusion.7
  320.3 2.8 multiply_reduce_fusion.7
  324.4 2.8 multiply_reduce_fusion.7
  328.5 2.8 multiply_reduce_fusion.7
  332.0 6.8 %convert_bitcast_fusion = bf16[8,512,256]{1,0,2:T(8,128)(2,1)S(1)} fusion(f32[512]{0:T(512)S(1)} %iota_convert_fusion, f32[16,256]{0,1:T(8,128)} %copy.22, f32[16,256]{0,1:T(8,128)S(1)} %copy-done.7, f32[16,256]{0,1:T(8,128)S(1)} %copy.23, f32[8]{0:T(128)S(1)} %maximum_convert_fusion.1, pred[8]{0:T(512)(128)(4,1)S(1)} %iota_compare_fusion.1), kind=kOutput, calls=%fused_computation.33 | convolution fusion | flops 206667776 | bytes 2148392 | tf_op jit(solution)/shard_map/inc,jnc->jic/dot_general | solution.py:175
  338.9 2.8 copy.26
  341.7 55.0 %reduce-scatter.5.cloned.1.call-done = bf16[512,256]{1,0:T(8,128)(2,1)} async-done(((bf16[4096,256]{1,0:T(8,128)(2,1)}), bf16[512,256]{1,0:T(8,128)(2,1)}) %reduce-scatter.5.cloned.1.call-update) | async-done | bytes 262160 | tf_op jit(solution)/shard_map/reduce_scatter | solution.py:174
  396.6 1.9 fusion.48
  (112 shorter events, 23.1 us)
Async XLA Ops:
  7.2 60.3 %copy-start = (bf16[512,256]{1,0:T(8,128)(2,1)S(1)}, bf16[512,256]{1,0:T(8,128)(2,1)}, u32[]{:S(2)}) copy-start(bf16[512,256]{1,0:T(8,128)(2,1)} %param.16) | copy-start | bytes 786436
  7.2 60.3 %all-gather.3.cloned.1.call-start = ((), (), s32[]{:S(2)}) async-start(), calls=%async_computation.2 | async-start | bytes 2359296 | tf_op jit(solution)/shard_map/all_gather | solution.py:94
  9.1 114.1 %all-gather.5.cloned.1.call-start = ((), (), s32[]{:S(2)}) async-start(), calls=%async_computation.3 | async-start | bytes 2359296 | tf_op jit(solution)/shard_map/all_gather | solution.py:95
  9.8 282.5 %reduce-scatter.3.cloned.1.call-start = ((), (), s32[]{:S(2)}) async-start(), calls=%async_computation.4 | async-start | bytes 8650752 | tf_op jit(solution)/shard_map/reduce_scatter | solution.py:147
  72.9 5.7 %copy-start.1 = (f32[2,512,4096]{2,1,0:T(8,128)}, f32[2,512,4096]{2,1,0:T(8,128)S(1)}, u32[]{:S(2)}) copy-start(f32[2,512,4096]{2,1,0:T(8,128)S(1)} %get-tuple-element.265) | copy-start | bytes 50331652
  138.1 0.7 copy-start.3
  138.1 258.5 %reduce-scatter.5.cloned.1.call-start = ((), (), s32[]{:S(2)}) async-start(), calls=%async_computation.5 | async-start | bytes 2359296 | tf_op jit(solution)/shard_map/reduce_scatter | solution.py:174
  216.2 76.1 %copy-start.5 = (bf16[512,256]{1,0:T(8,128)(2,1)S(1)}, bf16[512,256]{1,0:T(8,128)(2,1)}, u32[]{:S(2)}) copy-start(bf16[512,256]{1,0:T(8,128)(2,1)} %param.15) | copy-start | bytes 786436
  216.2 82.7 %copy-start.6 = (bf16[512,256]{1,0:T(8,128)(2,1)S(1)}, bf16[512,256]{1,0:T(8,128)(2,1)}, u32[]{:S(2)}) copy-start(bf16[512,256]{1,0:T(8,128)(2,1)} %param.20) | copy-start | bytes 786436
  293.4 5.8 %copy-start.2 = (bf16[512,256]{1,0:T(8,128)(2,1)}, bf16[512,256]{1,0:T(8,128)(2,1)S(1)}, u32[]{:S(2)}) copy-start(bf16[512,256]{1,0:T(8,128)(2,1)S(1)} %fusion.49) | copy-start | bytes 786436
  293.4 5.5 %collective-permute-start = (bf16[2,256]{1,0:T(2,128)(2,1)S(1)}, bf16[2,256]{1,0:T(2,128)(2,1)S(1)}, u32[]{:S(2)}, u32[]{:S(2)}) collective-permute-start(bf16[2,256]{1,0:T(2,128)(2,1)S(1)} %slice.28), channel_id=1, source_target_pairs={{0,32},{32,64},{64,96},{96,128},{128,160},{160,192},{192,224},{1,3... | collective-permute-start | bytes 3080 | tf_op jit(solution)/shard_map/ppermute | solution.py:14
  299.1 32.9 %copy-start.7 = (f32[16,256]{0,1:T(8,128)S(1)}, f32[16,256]{0,1:T(8,128)}, u32[]{:S(2)}) copy-start(f32[16,256]{0,1:T(8,128)} %copy.24) | copy-start | bytes 49156
  338.9 57.8 %copy-start.4 = (f32[8,64,256]{2,1,0:T(8,128)S(1)}, f32[8,64,256]{2,1,0:T(8,128)}, u32[]{:S(2)}) copy-start(f32[8,64,256]{2,1,0:T(8,128)} %get-tuple-element.105) | copy-start | bytes 1572868
  338.9 57.8 %copy-start.8 = (f32[256]{0:T(256)S(1)}, f32[256]{0:T(256)}, u32[]{:S(2)}) copy-start(f32[256]{0:T(256)} %param.25) | copy-start | bytes 3076
Sparse Core Ops, SparseCore 0:
  10.4 57.0 all-gather.2
  69.2 53.8 all-gather.4
  138.3 154.0 reduce-scatter.2
  341.8 54.8 reduce-scatter.4
where the time goes:
time: 406 us; the launch traced here: 405 us
  waiting for transfers between devices  227 us (56%)
  other arithmetic  125 us (31%)
  matrix products  27.2 us (7%)
  between operations  14 us (3%)
  local copies, waits for them, and re-layouts  8.16 us (2%)
    reduce_scatter x1, waiting for transfers between devices, per_device(): lax.psum_scatter(jnp.einsum('hqd,hdc->cq', heads_out, columns, preferred_...  72.1 us
    add x16, other arithmetic, add_pole(): total + residue[None, None, :] * jnp.exp(-rate[None, None, :] * safe_diff...  64.9 us
    reduce_scatter x1, waiting for transfers between devices, per_device(): lax.psum_scatter(jnp.einsum('inc,jnc->jic', long_powers, states, precisio...  55 us
    all_gather x1, waiting for transfers between devices, attend(): lax.all_gather(key_rows, 'ctx', axis=0, tiled=True)  54.2 us
    all_gather x1, waiting for transfers between devices, attend(): lax.all_gather(value_rows, 'ctx', axis=0, tiled=True)  44.5 us
    dot_general x8, other arithmetic, modal_step(): local = jnp.einsum('ijc,jc->ic', toeplitz, piece, precision=highest)  22.6 us
    dot_general x1, matrix products, per_device(): jnp.einsum('hqd,hdc->cq', heads_out, columns, preferred_element_type=jnp....  15 us
    neg x16, other arithmetic, add_pole(): -rate[None, None, :] * safe_diff[:, :, None]  11.3 us
  transfers between devices with their start and end apart: 5, of which 5 were waited for; matrix products, arithmetic and copies ran while one was open for 24% of the time, Pallas kernels for 0%

commit v1 on v0

--- a/solution.py
+++ b/solution.py
@@ -92,7 +92,9 @@
     )
     pieces = (
         lax.all_gather(key_rows, "ctx", axis=0, tiled=True),
-        lax.all_gather(value_rows, "ctx", axis=0, tiled=True),
+        jnp.concatenate(
+            lax.all_to_all(jnp.stack([value_rows] * lax.axis_size("ctx")), "ctx", 0, 0), axis=0
+        ),
     )
     count = pieces[0].shape[0]
     blocks = count // count

time: 406 us -> 377 us (0.929)
  waiting for transfers between devices: 227 us -> 201 us
  other arithmetic: 125 us -> 113 us
  starting transfers between devices: 3.65 us -> 9.3 us
  local copies, waits for them, and re-layouts: 8.16 us -> 12.4 us
    all_gather x1 -> x0, waiting for transfers between devices: 44.5 us -> none  [attend(): lax.all_gather(value_rows, 'ctx', axis=0, tiled=True)]
    all_to_all x0 -> x1, waiting for transfers between devices: none -> 33.2 us  [attend(): lax.all_to_all(jnp.stack([value_rows] * lax.axis_size('ctx')), 'ctx', 0, 0)]
    all_gather x1, waiting for transfers between devices: 54.2 us -> 26 us  [attend(): lax.all_gather(key_rows, 'ctx', axis=0, tiled=True)]
    reduce_scatter x1, waiting for transfers between devices: 72.1 us -> 85.3 us  [per_device(): lax.psum_scatter(jnp.einsum('hqd,hdc->cq', heads_out, columns, preferred_...]
    neg x16, other arithmetic: 11.3 us -> 0.11 us  [add_pole(): -rate[None, None, :] * safe_diff[:, :, None]]
    all_to_all x0 -> x1, starting transfers between devices: none -> 5.73 us  [attend(): lax.all_to_all(jnp.stack([value_rows] * lax.axis_size('ctx')), 'ctx', 0, 0)]
  transfers between devices with their start and end apart: 5 -> 5, of which waited for: 5 -> 5; matrix products, arithmetic and copies ran while one was open for 24% -> 21% of each run, Pallas kernels for 0% -> 0%
where the time goes in v1:
time: 377 us; the launch traced here: 376 us
  waiting for transfers between devices  201 us (53%)
  other arithmetic  113 us (30%)
  matrix products  26.6 us (7%)
  between operations  14 us (4%)
  local copies, waits for them, and re-layouts  12.4 us (3%)
  starting transfers between devices  9.3 us (2%)
    reduce_scatter x1, waiting for transfers between devices, per_device(): lax.psum_scatter(jnp.einsum('hqd,hdc->cq', heads_out, columns, preferred_...  85.3 us
    add x16, other arithmetic, add_pole(): total + residue[None, None, :] * jnp.exp(-rate[None, None, :] * safe_diff...  64.9 us
    reduce_scatter x1, waiting for transfers between devices, per_device(): lax.psum_scatter(jnp.einsum('inc,jnc->jic', long_powers, states, precisio...  54.6 us
    all_to_all x1, waiting for transfers between devices, attend(): lax.all_to_all(jnp.stack([value_rows] * lax.axis_size('ctx')), 'ctx', 0, 0)  33.2 us
    all_gather x1, waiting for transfers between devices, attend(): lax.all_gather(key_rows, 'ctx', axis=0, tiled=True)  26 us
    dot_general x8, other arithmetic, modal_step(): local = jnp.einsum('ijc,jc->ic', toeplitz, piece, precision=highest)  22.7 us
    dot_general x1, matrix products, per_device(): jnp.einsum('hqd,hdc->cq', heads_out, columns, preferred_element_type=jnp....  15.3 us
  transfers between devices with their start and end apart: 5, of which 5 were waited for; matrix products, arithmetic and copies ran while one was open for 21% of the time, Pallas kernels for 0%

profile of v1, /device:TPU:26, one launch (start us, length us, event | category | flops | bytes accessed | tf_op | source)
XLA Modules:
  0.0 376.5 jit_solution(12110629122724123308)
XLA Ops:
  7.2 1.8 copy.19
  9.1 2.4 stack.2
  11.5 5.7 %all-to-all-start = ((bf16[8,512,256]{2,1,0:T(8,128)(2,1)}), bf16[8,512,256]{2,1,0:T(8,128)(2,1)}, u32[]{:S(2)}, u32[]{:S(2)}) async-start(bf16[8,512,256]{2,1,0:T(8,128)(2,1)} %stack.2), calls=%async_computation | async-start | bytes 4194304 | tf_op jit(solution)/shard_map/all_to_all | solution.py:96
  17.4 1.7 iota_compare_fusion
  19.1 33.2 %all-to-all-done = bf16[8,512,256]{2,1,0:T(8,128)(2,1)} async-done(((bf16[8,512,256]{2,1,0:T(8,128)(2,1)}), bf16[8,512,256]{2,1,0:T(8,128)(2,1)}, u32[]{:S(2)}, u32[]{:S(2)}) %all-to-all-start) | async-done | bytes 2097184 | tf_op jit(solution)/shard_map/all_to_all | solution.py:96
  52.3 4.0 %squeeze.19 = bf16[4096,2,128]{2,1,0:T(2,128)(2,1)} reshape(bf16[8,512,256]{2,1,0:T(8,128)(2,1)} %all-to-all-done) | data formatting | bytes 4194304 | tf_op jit(solution)/shard_map/while/body/jit(dynamic_index_in_dim)/squeeze | solution.py:125
  56.3 26.0 %all-gather.2.cloned.1.call-done = bf16[4096,256]{0,1:T(8,128)(2,1)} async-done(((bf16[512,256]{0,1:T(8,128)(2,1)}), bf16[4096,256]{0,1:T(8,128)(2,1)}) %all-gather.2.cloned.1.call-update) | async-done | bytes 2097168 | tf_op jit(solution)/shard_map/all_gather | solution.py:94
  82.2 5.4 %fusion.6 = (f32[2,512]{1,0:T(2,128)S(1)}, f32[2,512,4096]{2,1,0:T(8,128)S(1)}) fusion(pred[512,4096]{1,0:T(8,128)(4,1)S(1)} %iota_compare_fusion, bf16[4096,2,128]{0,2,1:T(8,128)(2,1)} %bitcast.86, bf16[512,256]{1,0:T(8,128)(2,1)S(1)} %copy-done), kind=kOutput, calls=%fused_computation.17 | convolution fusion | flops 1086323712 | bytes 21237760 | tf_op jit(solution)/shard_map/while/body/eval_jaxpr/qhd,khd->hqk/dot_general | solution.py:66
  87.7 5.3 %fusion.7 = f32[2,512]{1,0:T(2,128)S(1)} fusion(f32[2,512,4096]{2,1,0:T(8,128)S(1)} %get-tuple-element.265, f32[2,512]{1,0:T(2,128)S(1)} %broadcast_maximum_fusion, pred[512,4096]{1,0:T(8,128)(4,1)S(1)} %iota_compare_fusion), kind=kLoop, calls=%fused_computation.18 | loop fusion | flops 20970496 | bytes 18882560 | tf_op jit(solution)/shard_map/while/body/eval_jaxpr/reduce_sum | solution.py:74
  93.4 15.3 %fusion.9 = bf16[8192,512]{0,1:T(8,128)(2,1)} fusion(bf16[2,128,8192]{2,1,0:T(8,128)(2,1)} %bitcast.85, bf16[4096,2,128]{2,1,0:T(2,128)(2,1)} %squeeze.19, f32[2,512,4096]{2,1,0:T(8,128)} %copy-done.1, f32[2,512]{1,0:T(2,128)S(1)} %broadcast_maximum_fusion, pred[512,4096]{1,0:T(8,128)(4,1)S(1)} %iota_compare_fusion, f32[2,512]{1,0:T(2,128)S(1)} %get-tuple-element.263, ...), kind=kOutput, calls=%fused_computation.20 | convolution fusion | flops 3246784512 | bytes 33566720 | tf_op jit(solution)/shard_map/hqd,hdc->cq/dot_general | solution.py:150
  108.8 0.6 copy-done.3
  109.4 66.4 %while.32 = (s32[]{:T(128)}, f32[64,64,256]{2,1,0:T(8,128)}, f32[16,256]{1,0:T(8,128)S(1)}, f32[16,256]{1,0:T(8,128)S(1)}, f32[64]{0:T(128)S(1)}, /*index=5*/s32[]{:T(128)}, s32[]{:T(128)}) while((s32[]{:T(128)}, f32[64,64,256]{2,1,0:T(8,128)}, f32[16,256]{1,0:T(8,128)S(1)}, f32[16,256]{1,0:T(8,128)S(1)}, f32[64]{0:T(128)S(1)}, ...), condition=%wide.region_4.5_spmd.clone, body=%wide.region_3.4_spmd.clone.sunk | while | flops 4202755 | bytes 8427867 | solution.py:31
  109.5 2.5 select_add_fusion.2
  112.1 4.1 %select_add_fusion.2 = f32[64,64,256]{2,1,0:T(8,128)} fusion(f32[64,64,256]{2,1,0:T(8,128)} %get-tuple-element.374, f32[64,64]{1,0:T(8,128)S(1)} %subtract_maximum_fusion.2, f32[256]{0:T(256)S(1)} %bitcast.80, f32[256]{0:T(256)S(1)} %bitcast.81, pred[]{:T(512)S(6)} %compare.8), kind=kLoop, calls=%fused_computation.3.clone.1 | loop fusion | flops 4194304 | bytes 8407041 | tf_op jit(solution)/shard_map/while/body/eval_jaxpr/add | solution.py:27
  116.2 4.1 %select_add_fusion.2 = f32[64,64,256]{2,1,0:T(8,128)} fusion(f32[64,64,256]{2,1,0:T(8,128)} %get-tuple-element.374, f32[64,64]{1,0:T(8,128)S(1)} %subtract_maximum_fusion.2, f32[256]{0:T(256)S(1)} %bitcast.80, f32[256]{0:T(256)S(1)} %bitcast.81, pred[]{:T(512)S(6)} %compare.8), kind=kLoop, calls=%fused_computation.3.clone.1 | loop fusion | flops 4194304 | bytes 8407041 | tf_op jit(solution)/shard_map/while/body/eval_jaxpr/add | solution.py:27
  120.4 4.1 %select_add_fusion.2 = f32[64,64,256]{2,1,0:T(8,128)} fusion(f32[64,64,256]{2,1,0:T(8,128)} %get-tuple-element.374, f32[64,64]{1,0:T(8,128)S(1)} %subtract_maximum_fusion.2, f32[256]{0:T(256)S(1)} %bitcast.80, f32[256]{0:T(256)S(1)} %bitcast.81, pred[]{:T(512)S(6)} %compare.8), kind=kLoop, calls=%fused_computation.3.clone.1 | loop fusion | flops 4194304 | bytes 8407041 | tf_op jit(solution)/shard_map/while/body/eval_jaxpr/add | solution.py:27
  124.6 4.3 %select_add_fusion.2 = f32[64,64,256]{2,1,0:T(8,128)} fusion(f32[64,64,256]{2,1,0:T(8,128)} %get-tuple-element.374, f32[64,64]{1,0:T(8,128)S(1)} %subtract_maximum_fusion.2, f32[256]{0:T(256)S(1)} %bitcast.80, f32[256]{0:T(256)S(1)} %bitcast.81, pred[]{:T(512)S(6)} %compare.8), kind=kLoop, calls=%fused_computation.3.clone.1 | loop fusion | flops 4194304 | bytes 8407041 | tf_op jit(solution)/shard_map/while/body/eval_jaxpr/add | solution.py:27
  128.9 4.3 %select_add_fusion.2 = f32[64,64,256]{2,1,0:T(8,128)} fusion(f32[64,64,256]{2,1,0:T(8,128)} %get-tuple-element.374, f32[64,64]{1,0:T(8,128)S(1)} %subtract_maximum_fusion.2, f32[256]{0:T(256)S(1)} %bitcast.80, f32[256]{0:T(256)S(1)} %bitcast.81, pred[]{:T(512)S(6)} %compare.8), kind=kLoop, calls=%fused_computation.3.clone.1 | loop fusion | flops 4194304 | bytes 8407041 | tf_op jit(solution)/shard_map/while/body/eval_jaxpr/add | solution.py:27
  133.3 4.3 %select_add_fusion.2 = f32[64,64,256]{2,1,0:T(8,128)} fusion(f32[64,64,256]{2,1,0:T(8,128)} %get-tuple-element.374, f32[64,64]{1,0:T(8,128)S(1)} %subtract_maximum_fusion.2, f32[256]{0:T(256)S(1)} %bitcast.80, f32[256]{0:T(256)S(1)} %bitcast.81, pred[]{:T(512)S(6)} %compare.8), kind=kLoop, calls=%fused_computation.3.clone.1 | loop fusion | flops 4194304 | bytes 8407041 | tf_op jit(solution)/shard_map/while/body/eval_jaxpr/add | solution.py:27
  137.7 4.3 %select_add_fusion.2 = f32[64,64,256]{2,1,0:T(8,128)} fusion(f32[64,64,256]{2,1,0:T(8,128)} %get-tuple-element.374, f32[64,64]{1,0:T(8,128)S(1)} %subtract_maximum_fusion.2, f32[256]{0:T(256)S(1)} %bitcast.80, f32[256]{0:T(256)S(1)} %bitcast.81, pred[]{:T(512)S(6)} %compare.8), kind=kLoop, calls=%fused_computation.3.clone.1 | loop fusion | flops 4194304 | bytes 8407041 | tf_op jit(solution)/shard_map/while/body/eval_jaxpr/add | solution.py:27
  142.0 4.3 %select_add_fusion.2 = f32[64,64,256]{2,1,0:T(8,128)} fusion(f32[64,64,256]{2,1,0:T(8,128)} %get-tuple-element.374, f32[64,64]{1,0:T(8,128)S(1)} %subtract_maximum_fusion.2, f32[256]{0:T(256)S(1)} %bitcast.80, f32[256]{0:T(256)S(1)} %bitcast.81, pred[]{:T(512)S(6)} %compare.8), kind=kLoop, calls=%fused_computation.3.clone.1 | loop fusion | flops 4194304 | bytes 8407041 | tf_op jit(solution)/shard_map/while/body/eval_jaxpr/add | solution.py:27
  146.4 4.3 %select_add_fusion.2 = f32[64,64,256]{2,1,0:T(8,128)} fusion(f32[64,64,256]{2,1,0:T(8,128)} %get-tuple-element.374, f32[64,64]{1,0:T(8,128)S(1)} %subtract_maximum_fusion.2, f32[256]{0:T(256)S(1)} %bitcast.80, f32[256]{0:T(256)S(1)} %bitcast.81, pred[]{:T(512)S(6)} %compare.8), kind=kLoop, calls=%fused_computation.3.clone.1 | loop fusion | flops 4194304 | bytes 8407041 | tf_op jit(solution)/shard_map/while/body/eval_jaxpr/add | solution.py:27
  150.7 4.2 %select_add_fusion.2 = f32[64,64,256]{2,1,0:T(8,128)} fusion(f32[64,64,256]{2,1,0:T(8,128)} %get-tuple-element.374, f32[64,64]{1,0:T(8,128)S(1)} %subtract_maximum_fusion.2, f32[256]{0:T(256)S(1)} %bitcast.80, f32[256]{0:T(256)S(1)} %bitcast.81, pred[]{:T(512)S(6)} %compare.8), kind=kLoop, calls=%fused_computation.3.clone.1 | loop fusion | flops 4194304 | bytes 8407041 | tf_op jit(solution)/shard_map/while/body/eval_jaxpr/add | solution.py:27
  155.1 4.1 %select_add_fusion.2 = f32[64,64,256]{2,1,0:T(8,128)} fusion(f32[64,64,256]{2,1,0:T(8,128)} %get-tuple-element.374, f32[64,64]{1,0:T(8,128)S(1)} %subtract_maximum_fusion.2, f32[256]{0:T(256)S(1)} %bitcast.80, f32[256]{0:T(256)S(1)} %bitcast.81, pred[]{:T(512)S(6)} %compare.8), kind=kLoop, calls=%fused_computation.3.clone.1 | loop fusion | flops 4194304 | bytes 8407041 | tf_op jit(solution)/shard_map/while/body/eval_jaxpr/add | solution.py:27
  159.2 4.1 %select_add_fusion.2 = f32[64,64,256]{2,1,0:T(8,128)} fusion(f32[64,64,256]{2,1,0:T(8,128)} %get-tuple-element.374, f32[64,64]{1,0:T(8,128)S(1)} %subtract_maximum_fusion.2, f32[256]{0:T(256)S(1)} %bitcast.80, f32[256]{0:T(256)S(1)} %bitcast.81, pred[]{:T(512)S(6)} %compare.8), kind=kLoop, calls=%fused_computation.3.clone.1 | loop fusion | flops 4194304 | bytes 8407041 | tf_op jit(solution)/shard_map/while/body/eval_jaxpr/add | solution.py:27
  163.4 4.1 %select_add_fusion.2 = f32[64,64,256]{2,1,0:T(8,128)} fusion(f32[64,64,256]{2,1,0:T(8,128)} %get-tuple-element.374, f32[64,64]{1,0:T(8,128)S(1)} %subtract_maximum_fusion.2, f32[256]{0:T(256)S(1)} %bitcast.80, f32[256]{0:T(256)S(1)} %bitcast.81, pred[]{:T(512)S(6)} %compare.8), kind=kLoop, calls=%fused_computation.3.clone.1 | loop fusion | flops 4194304 | bytes 8407041 | tf_op jit(solution)/shard_map/while/body/eval_jaxpr/add | solution.py:27
  167.6 4.1 %select_add_fusion.2 = f32[64,64,256]{2,1,0:T(8,128)} fusion(f32[64,64,256]{2,1,0:T(8,128)} %get-tuple-element.374, f32[64,64]{1,0:T(8,128)S(1)} %subtract_maximum_fusion.2, f32[256]{0:T(256)S(1)} %bitcast.80, f32[256]{0:T(256)S(1)} %bitcast.81, pred[]{:T(512)S(6)} %compare.8), kind=kLoop, calls=%fused_computation.3.clone.1 | loop fusion | flops 4194304 | bytes 8407041 | tf_op jit(solution)/shard_map/while/body/eval_jaxpr/add | solution.py:27
  171.7 4.1 %select_add_fusion.2 = f32[64,64,256]{2,1,0:T(8,128)} fusion(f32[64,64,256]{2,1,0:T(8,128)} %get-tuple-element.374, f32[64,64]{1,0:T(8,128)S(1)} %subtract_maximum_fusion.2, f32[256]{0:T(256)S(1)} %bitcast.80, f32[256]{0:T(256)S(1)} %bitcast.81, pred[]{:T(512)S(6)} %compare.8), kind=kLoop, calls=%fused_computation.3.clone.1 | loop fusion | flops 4194304 | bytes 8407041 | tf_op jit(solution)/shard_map/while/body/eval_jaxpr/add | solution.py:27
  175.8 4.0 %broadcast_select_fusion = f32[64,64,256]{2,1,0:T(8,128)} fusion(f32[64,64,256]{2,1,0:T(8,128)} %get-tuple-element.104, pred[64,64]{1,0:T(8,128)(4,1)S(1)} %subtract_compare_fusion), kind=kLoop, calls=%fused_computation.33 | loop fusion | flops 1048576 | bytes 8392704 | tf_op jit(solution)/shard_map/jit(_where)/select_n | solution.py:34
  179.8 85.3 %reduce-scatter.3.cloned.1.call-done = bf16[256,512]{0,1:T(8,128)(2,1)} async-done(((bf16[8192,512]{0,1:T(8,128)(2,1)}), bf16[256,512]{0,1:T(8,128)(2,1)}) %reduce-scatter.3.cloned.1.call-update) | async-done | bytes 262160 | tf_op jit(solution)/shard_map/reduce_scatter | solution.py:149
  265.0 1.0 fusion.48
  266.1 3.5 collective-permute-start
  269.8 1.7 collective-permute-done
  271.8 32.8 %while.33 = (s32[]{:T(128)}, f32[16,256]{1,0:T(8,128)S(1)}, f32[8,64,256]{2,1,0:T(8,128)}, f32[16,256]{1,0:T(8,128)S(1)}, f32[8,64,256]{2,1,0:T(8,128)S(1)}, /*i...) while((s32[]{:T(128)}, f32[16,256]{1,0:T(8,128)S(1)}, ...), condition=%wide.region_6.7_spmd.clone.clone.clone, body=%wide.region_5.6_spmd.clone.clone.clone.sunk | while | flops 3665923 | bytes 4949123 | solution.py:53
  272.5 2.8 multiply_reduce_fusion.7
  276.6 2.8 multiply_reduce_fusion.7
  280.7 2.8 multiply_reduce_fusion.7
  283.5 0.6 bitcast_dynamic-update-slice_fusion.2
  284.8 2.8 multiply_reduce_fusion.7
  288.9 2.8 multiply_reduce_fusion.7
  293.0 2.8 multiply_reduce_fusion.7
  297.1 2.8 multiply_reduce_fusion.7
  299.9 0.6 bitcast_dynamic-update-slice_fusion.2
  301.2 2.8 multiply_reduce_fusion.7
  304.7 5.9 %convert_bitcast_fusion = bf16[8,512,256]{1,0,2:T(8,128)(2,1)S(1)} fusion(f32[512]{0:T(512)S(1)} %iota_convert_fusion, f32[16,256]{0,1:T(8,128)S(1)} %copy.22, f32[16,256]{0,1:T(8,128)S(1)} %copy.24, f32[16,256]{0,1:T(8,128)S(1)} %copy.23, f32[8]{0:T(128)S(1)} %maximum_convert_fusion.1, pred[8]{0:T(512)(128)(4,1)S(1)} %iota_compare_fusion.1), kind=kOutput, calls=%fused_computation.32 | convolution fusion | flops 206667776 | bytes 2148392 | tf_op jit(solution)/shard_map/inc,jnc->jic/dot_general | solution.py:177
  310.6 2.8 copy.26
  313.4 54.6 %reduce-scatter.5.cloned.1.call-done = bf16[512,256]{1,0:T(8,128)(2,1)} async-done(((bf16[4096,256]{1,0:T(8,128)(2,1)}), bf16[512,256]{1,0:T(8,128)(2,1)}) %reduce-scatter.5.cloned.1.call-update) | async-done | bytes 262160 | tf_op jit(solution)/shard_map/reduce_scatter | solution.py:176
  368.0 1.9 fusion.47
  (115 shorter events, 11.2 us)
Async XLA Ops:
  7.2 75.1 %copy-start = (bf16[512,256]{1,0:T(8,128)(2,1)S(1)}, bf16[512,256]{1,0:T(8,128)(2,1)}, u32[]{:S(2)}) copy-start(bf16[512,256]{1,0:T(8,128)(2,1)} %param.16) | copy-start | bytes 786436
  7.2 10.1 %copy-start.8 = (f32[3,256]{1,0:T(4,128)S(1)}, f32[3,256]{1,0:T(4,128)}, u32[]{:S(2)}) copy-start(f32[3,256]{1,0:T(4,128)} %param.22) | copy-start | bytes 9220
  7.2 10.2 %copy-start.7 = (f32[16,256]{1,0:T(8,128)S(1)}, f32[16,256]{1,0:T(8,128)}, u32[]{:S(2)}) copy-start(f32[16,256]{1,0:T(8,128)} %param.23) | copy-start | bytes 49156
  7.2 75.0 %all-gather.2.cloned.1.call-start = ((), (), s32[]{:S(2)}) async-start(), calls=%async_computation.3 | async-start | bytes 2359296 | tf_op jit(solution)/shard_map/all_gather | solution.py:94
  11.5 40.8 %all-to-all-start = ((bf16[8,512,256]{2,1,0:T(8,128)(2,1)}), bf16[8,512,256]{2,1,0:T(8,128)(2,1)}, u32[]{:S(2)}, u32[]{:S(2)}) async-start(bf16[8,512,256]{2,1,0:T(8,128)(2,1)} %stack.2), calls=%async_computation | async-start | bytes 4194304 | tf_op jit(solution)/shard_map/all_to_all | solution.py:96
  17.2 247.8 %reduce-scatter.3.cloned.1.call-start = ((), (), s32[]{:S(2)}) async-start(), calls=%async_computation.4 | async-start | bytes 8650752 | tf_op jit(solution)/shard_map/reduce_scatter | solution.py:149
  87.7 5.7 %copy-start.1 = (f32[2,512,4096]{2,1,0:T(8,128)}, f32[2,512,4096]{2,1,0:T(8,128)S(1)}, u32[]{:S(2)}) copy-start(f32[2,512,4096]{2,1,0:T(8,128)S(1)} %get-tuple-element.265) | copy-start | bytes 50331652
  108.7 0.7 copy-start.3
  108.7 259.3 %reduce-scatter.5.cloned.1.call-start = ((), (), s32[]{:S(2)}) async-start(), calls=%async_computation.5 | async-start | bytes 2359296 | tf_op jit(solution)/shard_map/reduce_scatter | solution.py:176
  175.8 89.2 %copy-start.5 = (bf16[512,256]{1,0:T(8,128)(2,1)S(1)}, bf16[512,256]{1,0:T(8,128)(2,1)}, u32[]{:S(2)}) copy-start(bf16[512,256]{1,0:T(8,128)(2,1)} %param.15) | copy-start | bytes 786436
  175.8 95.8 %copy-start.6 = (bf16[512,256]{1,0:T(8,128)(2,1)S(1)}, bf16[512,256]{1,0:T(8,128)(2,1)}, u32[]{:S(2)}) copy-start(bf16[512,256]{1,0:T(8,128)(2,1)} %param.20) | copy-start | bytes 786436
  266.0 5.8 %copy-start.2 = (bf16[512,256]{1,0:T(8,128)(2,1)}, bf16[512,256]{1,0:T(8,128)(2,1)S(1)}, u32[]{:S(2)}) copy-start(bf16[512,256]{1,0:T(8,128)(2,1)S(1)} %fusion.48) | copy-start | bytes 786436
  266.1 5.5 %collective-permute-start = (bf16[2,256]{1,0:T(2,128)(2,1)S(1)}, bf16[2,256]{1,0:T(2,128)(2,1)S(1)}, u32[]{:S(2)}, u32[]{:S(2)}) collective-permute-start(bf16[2,256]{1,0:T(2,128)(2,1)S(1)} %slice.28), channel_id=1, source_target_pairs={{0,32},{32,64},{64,96},{96,128},{128,160},{160,192},{192,224},{1,3... | collective-permute-start | bytes 3080 | tf_op jit(solution)/shard_map/ppermute | solution.py:14
  310.6 57.4 %copy-start.4 = (f32[8,64,256]{2,1,0:T(8,128)S(1)}, f32[8,64,256]{2,1,0:T(8,128)}, u32[]{:S(2)}) copy-start(f32[8,64,256]{2,1,0:T(8,128)} %get-tuple-element.105) | copy-start | bytes 1572868
  310.6 57.4 %copy-start.9 = (f32[256]{0:T(256)S(1)}, f32[256]{0:T(256)}, u32[]{:S(2)}) copy-start(f32[256]{0:T(256)} %param.25) | copy-start | bytes 3076
Sparse Core Ops, SparseCore 0:
  10.4 71.8 all-gather.1
  108.8 156.1 reduce-scatter.2
  313.6 54.4 reduce-scatter.4
